TPU v7x, 32 devices: a whole 2x2x4 slice. The times are simulated.
32 devices in a mesh: expert: 16 (over z, y, x), dp: 2 (over core).
Axes of the slice: x: 2, y: 2, z: 4, core: 2. Of those that a mesh axis runs over, the one named last changes fastest.
Arguments:
- tokens: bfloat16 [512, 7168], P('expert', 'dp'), may hold values from -6 to 6
- cotangent: bfloat16 [512, 7168], P('expert', 'dp'), may hold values from -6 to 6
- expert_ids: int32 [512, 8], P('expert'), may hold values from 0 to 15, all different within a row; in each aligned block of 32 rows (0 to 31, 32 to 63, ...) at most 32 rows name the same one
- route_weight: float32 [512, 8], P('expert'), may hold values from 0.1 to 1
- gate_weight: bfloat16 [16, 7168, 1024], P('expert', 'dp'), may hold values from -0.0625 to 0.0625
- up_weight: bfloat16 [16, 7168, 1024], P('expert', 'dp'), may hold values from -0.0625 to 0.0625
- down_weight: bfloat16 [16, 7168, 1024], P('expert', 'dp'), may hold values from -0.1875 to 0.1875
Outputs:
- mixed: bfloat16 [512, 7168], P('expert', 'dp')
- grad_tokens: bfloat16 [512, 7168], P('expert', 'dp')
Inputs may be any that keep to these rules, and one draw needn't show every extreme that they name: `expert_ids`: each row names 8 different experts. In the rows of one device (aligned blocks of 32 rows) no expert is named more than 32 times, and in every draw some block names some expert exactly 32 times.
All inputs are finite; a program needn't handle non-finite values.
Results may differ from a plain program's by a relative error of at most 0.028.
Values may be sent and summed in bfloat16 or wider, within the bound.
No kernel may reach another device: no remote copies, remote signals or barrier semaphores. Data moves between devices by JAX's collectives and lax.ppermute only.
A program may use at most 64 MiB of HBM per device.

v0:
```python
import jax
import jax.numpy as jnp
from jax import lax
from jax.sharding import PartitionSpec as P


def local(tokens, cotangent, expert_ids, route_weight, gate_weight, up_weight, down_weight):
    f32, bf16 = (jnp.float32, jnp.bfloat16)
    me = lax.axis_index("expert")
    gate_w = gate_weight[0]
    up_w = up_weight[0]
    down_w = down_weight[0]
    all_tokens = lax.all_gather(tokens, "expert", axis=0, tiled=True)
    all_cot = lax.all_gather(cotangent, "expert", axis=0, tiled=True)
    all_ids = lax.all_gather(expert_ids, "expert", axis=0, tiled=True)
    all_weight = lax.all_gather(route_weight, "expert", axis=0, tiled=True)
    chosen = all_ids == me
    weight = jnp.sum(jnp.where(chosen, all_weight, 0.0), axis=1, keepdims=True)
    named = jnp.any(chosen, axis=1, keepdims=True)
    gate_part = jnp.dot(all_tokens, gate_w, preferred_element_type=f32).astype(bf16)
    up_part = jnp.dot(all_tokens, up_w, preferred_element_type=f32).astype(bf16)
    hidden_part = (weight * jnp.dot(all_cot, down_w, preferred_element_type=f32)).astype(bf16)
    gate = lax.psum(gate_part, "dp").astype(f32)
    up = lax.psum(up_part, "dp").astype(f32)
    hidden_grad = lax.psum(hidden_part, "dp").astype(f32)
    sig = jax.nn.sigmoid(gate)
    hidden = (gate * sig * up).astype(bf16)
    up_grad = (hidden_grad * gate * sig).astype(bf16)
    gate_grad = (hidden_grad * up * sig * (1.0 + gate * (1.0 - sig))).astype(bf16)
    contract = (((1,), (1,)), ((), ()))
    out = (weight * lax.dot_general(hidden, down_w, contract, preferred_element_type=f32)).astype(
        bf16
    )
    grad = lax.dot_general(
        gate_grad, gate_w, contract, preferred_element_type=f32
    ) + lax.dot_general(up_grad, up_w, contract, preferred_element_type=f32)
    grad = jnp.where(named, grad, 0.0).astype(bf16)
    mixed = lax.psum_scatter(out, "expert", scatter_dimension=0, tiled=True)
    grad_tokens = lax.psum_scatter(grad, "expert", scatter_dimension=0, tiled=True)
    return (mixed, grad_tokens)


def solution(mesh):
    return jax.shard_map(
        local,
        mesh=mesh,
        in_specs=(
            P("expert", "dp"),
            P("expert", "dp"),
            P("expert", None),
            P("expert", None),
            P("expert", "dp", None),
            P("expert", "dp", None),
            P("expert", "dp", None),
        ),
        out_specs=(P("expert", "dp"), P("expert", "dp")),
        check_vma=False,
    )
```

profile of v0, /device:TPU:0, one launch (start us, length us, event | category | flops | bytes accessed | tf_op | source)
XLA Modules:
  0.0 392.5 jit_solution(4316116910010661094)
XLA Ops:
  7.2 0.0 all-gather.5.cloned.1.call-start
  7.2 0.7 all-gather.5.cloned.1.call-update
  7.9 0.0 all-gather.7.cloned.1.call-start
  7.9 0.7 all-gather.7.cloned.1.call-update
  8.6 0.0 all-reduce.3.cloned.1.call-start
  8.7 43.4 %all-gather = s32[16,32,8]{1,2,0:T(8,128)S(1)} all-gather(s32[1,32,8]{1,2,0:T(8,128)} %bitcast.30), channel_id=1, replica_groups=mesh['expert'=16,'dp'=2] {'expert'}, dimensions={0}, use_global_device_ids=true | all-gather | bytes 17408 | tf_op jit(solution)/shard_map/all_gather | solution.py:15
  52.1 37.4 %all-gather.1 = f32[16,32,8]{1,2,0:T(8,128)S(1)} all-gather(f32[1,32,8]{1,2,0:T(8,128)} %bitcast.31), channel_id=1, replica_groups=mesh['expert'=16,'dp'=2] {'expert'}, dimensions={0}, use_global_device_ids=true | all-gather | bytes 17408 | tf_op jit(solution)/shard_map/all_gather | solution.py:16
  89.6 0.1 reshape.15
  89.6 0.0 all-gather.5.cloned.1.call-done
  89.6 0.0 copy-start
  89.6 9.3 %fusion.28 = bf16[512,1024]{1,0:T(8,128)(2,1)} fusion(bf16[512,3584]{1,0:T(8,128)(2,1)} %all-gather.5.cloned.1.call-done, bf16[1,3584,1024]{2,1,0:T(8,128)(2,1)} %param.11), kind=kOutput, calls=%fused_computation.31 | convolution fusion | flops 3758620672 | bytes 12058624 | tf_op jit(solution)/shard_map/dot_general | solution.py:20
  98.9 0.0 copy-done
  98.9 7.4 %fusion.31 = bf16[512,1024]{1,0:T(8,128)(2,1)} fusion(bf16[512,3584]{1,0:T(8,128)(2,1)S(1)} %copy-done, bf16[1,3584,1024]{2,1,0:T(8,128)(2,1)} %param.12), kind=kOutput, calls=%fused_computation.32 | convolution fusion | flops 3758620672 | bytes 12058624 | tf_op jit(solution)/shard_map/dot_general | solution.py:21
  106.3 52.5 %all-gather.7.cloned.1.call-done = bf16[512,3584]{1,0:T(8,128)(2,1)} async-done(((bf16[32,3584]{1,0:T(8,128)(2,1)}), bf16[512,3584]{1,0:T(8,128)(2,1)}) %all-gather.7.cloned.1.call-update) | async-done | bytes 3670032 | tf_op jit(solution)/shard_map/all_gather | solution.py:14
  158.8 9.2 %multiply_convert_fusion.1 = bf16[512,1024]{1,0:T(8,128)(2,1)} fusion(bf16[512,3584]{1,0:T(8,128)(2,1)} %all-gather.7.cloned.1.call-done, bf16[1,3584,1024]{2,1,0:T(8,128)(2,1)} %param.13, f32[512]{0:T(512)S(1)} %reshape.15), kind=kOutput, calls=%fused_computation.30 | convolution fusion | flops 3759144960 | bytes 12060672 | tf_op jit(solution)/shard_map/dot_general | solution.py:22
  168.0 0.0 all-reduce.3.cloned.1.call-update
  168.0 0.2 reduce-scatter.5.cloned.1.call-start
  168.2 0.1 reshape.12
  168.3 21.9 %all-reduce.3.cloned.1.call-done = (bf16[512,1024]{1,0:T(8,128)(2,1)}, bf16[512,1024]{1,0:T(8,128)(2,1)}, bf16[512,1024]{1,0:T(8,128)(2,1)}) async-done(((bf16[512,1024]{1,0:T(8,128)(2,1)}, bf16[512,1024]{1,0:T(8,128)(2,1)}, bf16[512,1024]{1,0:T(8,128)(2,1)}), (bf16[512,1024]{1,0:T(8,128)(2,1)}, bf16[512,1024]{1,0:T(8,128)(2,1)}, bf16[512,1024]{1,0:T(8,128)(2,1)})) %all-reduce.3.cloned.1.call-update) | async-done | bytes 3145744 | tf_op jit(solution)/shard_map/psum | solution.py:24
  190.2 0.0 copy-start.1
  190.2 0.0 copy-start.2
  190.2 0.0 copy-start.3
  190.2 10.9 %fusion.4 = f32[512,3584]{1,0:T(8,128)} fusion(bf16[1,3584,1024]{2,1,0:T(8,128)(2,1)} %param.12, bf16[512,1024]{1,0:T(8,128)(2,1)} %get-tuple-element.3, bf16[512,1024]{1,0:T(8,128)(2,1)} %get-tuple-element.4), kind=kOutput, calls=%fused_computation.4 | convolution fusion | flops 3762290688 | bytes 16777216 | tf_op jit(solution)/shard_map/dot_general | solution.py:36
  201.1 0.0 copy-done.1
  201.1 0.0 copy-done.2
  201.2 0.0 copy-done.3
  201.2 10.3 %select_convert_fusion = bf16[512,3584]{1,0:T(8,128)(2,1)} fusion(f32[512,3584]{1,0:T(8,128)} %fusion.4, bf16[1,3584,1024]{2,1,0:T(8,128)(2,1)} %param.11, pred[512]{0:T(512)(128)(4,1)S(1)} %reshape.12, bf16[512,1024]{1,0:T(8,128)(2,1)S(1)} %copy-done.1, bf16[512,1024]{1,0:T(8,128)(2,1)S(1)} %copy-done.3, bf16[512,1024]{1,0:T(8,128)(2,1)S(1)} %copy-done.2), kind=kOutput, calls=%fused_computation.12 | convolution fusion | flops 3770417152 | bytes 21496320 | tf_op jit(solution)/shard_map/dot_general | solution.py:34
  211.5 0.0 reduce-scatter.5.cloned.1.call-update
  211.5 0.0 reduce-scatter.3.cloned.1.call-start
  211.5 8.8 %multiply_convert_fusion = bf16[512,3584]{1,0:T(8,128)(2,1)} fusion(bf16[1,3584,1024]{2,1,0:T(8,128)(2,1)} %param.13, f32[512]{0:T(512)S(1)} %reshape.15, bf16[512,1024]{1,0:T(8,128)(2,1)S(1)} %copy-done.1, bf16[512,1024]{1,0:T(8,128)(2,1)S(1)} %copy-done.2), kind=kOutput, calls=%fused_computation.13 | convolution fusion | flops 3765960704 | bytes 13109248 | tf_op jit(solution)/shard_map/dot_general | solution.py:31
  220.3 0.0 reduce-scatter.3.cloned.1.call-update
  220.3 78.2 %reduce-scatter.5.cloned.1.call-done = bf16[32,3584]{1,0:T(8,128)(2,1)} async-done(((bf16[512,3584]{1,0:T(8,128)(2,1)}), bf16[32,3584]{1,0:T(8,128)(2,1)}) %reduce-scatter.5.cloned.1.call-update) | async-done | bytes 229392 | tf_op jit(solution)/shard_map/reduce_scatter | solution.py:39
  298.5 87.5 %reduce-scatter.3.cloned.1.call-done = bf16[32,3584]{1,0:T(8,128)(2,1)} async-done(((bf16[512,3584]{1,0:T(8,128)(2,1)}), bf16[32,3584]{1,0:T(8,128)(2,1)}) %reduce-scatter.3.cloned.1.call-update) | async-done | bytes 229392 | tf_op jit(solution)/shard_map/reduce_scatter | solution.py:38
  (2 shorter events, 0.1 us)
Async XLA Ops:
  7.2 82.5 %all-gather.5.cloned.1.call-start = ((), (), s32[]{:S(2)}) async-start(), calls=%async_computation.2 | async-start | bytes 3899392 | tf_op jit(solution)/shard_map/all_gather | solution.py:13
  7.9 150.9 %all-gather.7.cloned.1.call-start = ((), (), s32[]{:S(2)}) async-start(), calls=%async_computation.4 | async-start | bytes 3899392 | tf_op jit(solution)/shard_map/all_gather | solution.py:14
  8.6 181.6 %all-reduce.3.cloned.1.call-start = ((), (), s32[]{:S(2)}) async-start(), calls=%async_computation.6 | async-start | bytes 6291456 | tf_op jit(solution)/shard_map/psum | solution.py:24
  89.6 9.3 %copy-start = (bf16[512,3584]{1,0:T(8,128)(2,1)S(1)}, bf16[512,3584]{1,0:T(8,128)(2,1)}, u32[]{:S(2)}) copy-start(bf16[512,3584]{1,0:T(8,128)(2,1)} %all-gather.5.cloned.1.call-done) | copy-start | bytes 11010052
  168.0 130.5 %reduce-scatter.5.cloned.1.call-start = ((), (), s32[]{:S(2)}) async-start(), calls=%async_computation.5 | async-start | bytes 3899392 | tf_op jit(solution)/shard_map/reduce_scatter | solution.py:39
  190.2 10.9 %copy-start.1 = (bf16[512,1024]{1,0:T(8,128)(2,1)S(1)}, bf16[512,1024]{1,0:T(8,128)(2,1)}, u32[]{:S(2)}) copy-start(bf16[512,1024]{1,0:T(8,128)(2,1)} %get-tuple-element.2) | copy-start | bytes 3145732
  190.2 10.9 %copy-start.2 = (bf16[512,1024]{1,0:T(8,128)(2,1)S(1)}, bf16[512,1024]{1,0:T(8,128)(2,1)}, u32[]{:S(2)}) copy-start(bf16[512,1024]{1,0:T(8,128)(2,1)} %get-tuple-element.3) | copy-start | bytes 3145732
  190.2 10.9 %copy-start.3 = (bf16[512,1024]{1,0:T(8,128)(2,1)S(1)}, bf16[512,1024]{1,0:T(8,128)(2,1)}, u32[]{:S(2)}) copy-start(bf16[512,1024]{1,0:T(8,128)(2,1)} %get-tuple-element.4) | copy-start | bytes 3145732
  211.5 174.5 %reduce-scatter.3.cloned.1.call-start = ((), (), s32[]{:S(2)}) async-start(), calls=%async_computation.3 | async-start | bytes 3899392 | tf_op jit(solution)/shard_map/reduce_scatter | solution.py:38
Sparse Core Ops, SparseCore 0:
  10.7 74.9 all-gather.4
  88.5 70.2 all-gather.6
  168.1 22.0 all-reduce.2
  211.6 86.8 reduce-scatter.4
  301.3 84.6 reduce-scatter.2
where the time goes:
time: 393 us
  waiting for transfers between devices  241 us (61%)
  blocking collectives  80.8 us (21%)
  matrix products  55.9 us (14%)
  between operations  13.8 us (4%)
    reduce_scatter x1, waiting for transfers between devices, local(): mixed = lax.psum_scatter(out, 'expert', scatter_dimension=0, tiled=True)  87.5 us
    reduce_scatter x1, waiting for transfers between devices, local(): lax.psum_scatter(grad, 'expert', scatter_dimension=0, tiled=True)  78.2 us
    all_gather x1, waiting for transfers between devices, local(): all_cot = lax.all_gather(cotangent, 'expert', axis=0, tiled=True)  52.5 us
    all_gather x1, blocking collectives, local(): all_ids = lax.all_gather(expert_ids, 'expert', axis=0, tiled=True)  43.4 us
    all_gather x1, blocking collectives, local(): all_weight = lax.all_gather(route_weight, 'expert', axis=0, tiled=True)  37.4 us
    psum x1, waiting for transfers between devices, local(): up = lax.psum(up_part, 'dp').astype(f32)  21.9 us
    dot_general x1, matrix products, local(): lax.dot_general(up_grad, up_w, contract, preferred_element_type=f32)  10.9 us
    dot_general x1, matrix products, local(): lax.dot_general(gate_grad, gate_w, contract, preferred_element_type=f32)  10.3 us
  transfers between devices with their start and end apart: 5, of which 4 were waited for; matrix products, arithmetic and copies ran while one was open for 7% of the time, Pallas kernels for 0%

commit v1 on v0

--- a/solution.py
+++ b/solution.py
@@ -12,7 +12,13 @@
     down_w = down_weight[0]
     all_tokens = lax.all_gather(tokens, "expert", axis=0, tiled=True)
     all_cot = lax.all_gather(cotangent, "expert", axis=0, tiled=True)
-    all_ids = lax.all_gather(expert_ids, "expert", axis=0, tiled=True)
+    x = expert_ids
+    ways, here, step = (lax.axis_size("expert"), lax.axis_index("expert"), x.shape[0])
+    lengths = [n * ways if d == 0 else n for d, n in enumerate(x.shape)]
+    all_ids = lax.dynamic_update_slice_in_dim(jnp.zeros(lengths, x.dtype), x, here * step, axis=0)
+    for far in range(1, ways):
+        x = lax.ppermute(x, "expert", [(d, (d + 1) % ways) for d in range(ways)])
+        all_ids = lax.dynamic_update_slice_in_dim(all_ids, x, (here - far) % ways * step, axis=0)
     all_weight = lax.all_gather(route_weight, "expert", axis=0, tiled=True)
     chosen = all_ids == me
     weight = jnp.sum(jnp.where(chosen, all_weight, 0.0), axis=1, keepdims=True)

time: 393 us -> 394 us (level)
  blocking collectives: 80.8 us -> 40.5 us
  waiting for transfers between devices: 241 us -> 275 us
  local copies, waits for them, and re-layouts: 0.18 us -> 4.85 us
    ppermute x0 -> x15, waiting for transfers between devices: none -> 97.1 us  [local(): x = lax.ppermute(x, 'expert', [(d, (d + 1) % ways) for d in range(ways)])]
    all_gather x1, waiting for transfers between devices: 52.5 us -> 0.01 us  [local(): all_cot = lax.all_gather(cotangent, 'expert', axis=0, tiled=True)]
    all_gather x1 -> x0, blocking collectives: 43.4 us -> none  [local(): all_ids = lax.all_gather(expert_ids, 'expert', axis=0, tiled=True)]
    reduce_scatter x1, waiting for transfers between devices: 87.5 us -> 67 us  [local(): mixed = lax.psum_scatter(out, 'expert', scatter_dimension=0, tiled=True)]
    reduce_scatter x1, waiting for transfers between devices: 78.2 us -> 87.3 us  [local(): lax.psum_scatter(grad, 'expert', scatter_dimension=0, tiled=True)]
    dynamic_update_slice x0 -> x16, local copies, waits for them, and re-layouts: none -> 4.72 us  [the longest x15 3.94 us: local(): lax.dynamic_update_slice_in_dim(all_ids, x, (here - far) % ways * step, a...]
  transfers between devices with their start and end apart: 5 -> 20, of which waited for: 4 -> 17; matrix products, arithmetic and copies ran while one was open for 7% -> 11% of each run, Pallas kernels for 0% -> 0%
where the time goes in v1:
time: 394 us
  waiting for transfers between devices  275 us (70%)
  matrix products  55.7 us (14%)
  blocking collectives  40.5 us (10%)
  between operations  14 us (4%)
  local copies, waits for them, and re-layouts  4.85 us (1%)
    ppermute x15, waiting for transfers between devices, local(): x = lax.ppermute(x, 'expert', [(d, (d + 1) % ways) for d in range(ways)])  97.1 us
    reduce_scatter x1, waiting for transfers between devices, local(): lax.psum_scatter(grad, 'expert', scatter_dimension=0, tiled=True)  87.3 us
    reduce_scatter x1, waiting for transfers between devices, local(): mixed = lax.psum_scatter(out, 'expert', scatter_dimension=0, tiled=True)  67 us
    all_gather x1, blocking collectives, local(): all_weight = lax.all_gather(route_weight, 'expert', axis=0, tiled=True)  40.5 us
    psum x1, waiting for transfers between devices, local(): up = lax.psum(up_part, 'dp').astype(f32)  22.3 us
    dot_general x1, matrix products, local(): lax.dot_general(gate_grad, gate_w, contract, preferred_element_type=f32)  11.6 us
    dot_general x1, matrix products, local(): lax.dot_general(hidden, down_w, contract, preferred_element_type=f32)  9.84 us
    dot_general x1, matrix products, local(): up_part = jnp.dot(all_tokens, up_w, preferred_element_type=f32).astype(bf16)  9.35 us
  transfers between devices with their start and end apart: 20, of which 17 were waited for; matrix products, arithmetic and copies ran while one was open for 11% of the time, Pallas kernels for 0%

profile of v1, /device:TPU:0, one launch (start us, length us, event | category | flops | bytes accessed | tf_op | source)
XLA Modules:
  0.0 393.6 jit_solution(7852412366992350281)
XLA Ops:
  7.2 0.7 all-gather.4.cloned.1.call-update
  7.9 0.0 all-gather.6.cloned.1.call-start
  7.9 0.7 all-gather.6.cloned.1.call-update
  8.6 0.0 all-reduce.3.cloned.1.call-start
  8.7 3.0 collective-permute-start
  11.7 40.5 %all-gather = f32[16,32,8]{1,2,0:T(8,128)S(1)} all-gather(f32[1,32,8]{1,2,0:T(8,128)} %bitcast.31), channel_id=1, replica_groups=mesh['expert'=16,'dp'=2] {'expert'}, dimensions={0}, use_global_device_ids=true | all-gather | bytes 17408 | tf_op jit(solution)/shard_map/all_gather | solution.py:22
  52.2 7.2 %collective-permute-done.1 = s32[32,8]{0,1:T(8,128)S(1)} collective-permute-done((s32[32,8]{0,1:T(8,128)S(1)}, s32[32,8]{0,1:T(8,128)S(1)}, u32[]{:S(2)}, u32[]{:S(2)}) %collective-permute-start.1) | collective-permute-done | bytes 1056 | tf_op jit(solution)/shard_map/ppermute | solution.py:20
  59.4 7.3 %collective-permute-done.2 = s32[32,8]{0,1:T(8,128)S(1)} collective-permute-done((s32[32,8]{0,1:T(8,128)S(1)}, s32[32,8]{0,1:T(8,128)S(1)}, u32[]{:S(2)}, u32[]{:S(2)}) %collective-permute-start.2) | collective-permute-done | bytes 1056 | tf_op jit(solution)/shard_map/ppermute | solution.py:20
  66.7 7.4 %collective-permute-done.3 = s32[32,8]{0,1:T(8,128)S(1)} collective-permute-done((s32[32,8]{0,1:T(8,128)S(1)}, s32[32,8]{0,1:T(8,128)S(1)}, u32[]{:S(2)}, u32[]{:S(2)}) %collective-permute-start.3) | collective-permute-done | bytes 1056 | tf_op jit(solution)/shard_map/ppermute | solution.py:20
  74.2 7.2 %collective-permute-done.4 = s32[32,8]{0,1:T(8,128)S(1)} collective-permute-done((s32[32,8]{0,1:T(8,128)S(1)}, s32[32,8]{0,1:T(8,128)S(1)}, u32[]{:S(2)}, u32[]{:S(2)}) %collective-permute-start.4) | collective-permute-done | bytes 1056 | tf_op jit(solution)/shard_map/ppermute | solution.py:20
  81.4 7.2 %collective-permute-done.5 = s32[32,8]{0,1:T(8,128)S(1)} collective-permute-done((s32[32,8]{0,1:T(8,128)S(1)}, s32[32,8]{0,1:T(8,128)S(1)}, u32[]{:S(2)}, u32[]{:S(2)}) %collective-permute-start.5) | collective-permute-done | bytes 1056 | tf_op jit(solution)/shard_map/ppermute | solution.py:20
  88.6 7.2 %collective-permute-done.6 = s32[32,8]{0,1:T(8,128)S(1)} collective-permute-done((s32[32,8]{0,1:T(8,128)S(1)}, s32[32,8]{0,1:T(8,128)S(1)}, u32[]{:S(2)}, u32[]{:S(2)}) %collective-permute-start.6) | collective-permute-done | bytes 1056 | tf_op jit(solution)/shard_map/ppermute | solution.py:20
  95.8 7.2 %collective-permute-done.7 = s32[32,8]{0,1:T(8,128)S(1)} collective-permute-done((s32[32,8]{0,1:T(8,128)S(1)}, s32[32,8]{0,1:T(8,128)S(1)}, u32[]{:S(2)}, u32[]{:S(2)}) %collective-permute-start.7) | collective-permute-done | bytes 1056 | tf_op jit(solution)/shard_map/ppermute | solution.py:20
  103.0 7.2 %collective-permute-done.8 = s32[32,8]{0,1:T(8,128)S(1)} collective-permute-done((s32[32,8]{0,1:T(8,128)S(1)}, s32[32,8]{0,1:T(8,128)S(1)}, u32[]{:S(2)}, u32[]{:S(2)}) %collective-permute-start.8) | collective-permute-done | bytes 1056 | tf_op jit(solution)/shard_map/ppermute | solution.py:20
  110.2 7.3 %collective-permute-done.9 = s32[32,8]{0,1:T(8,128)S(1)} collective-permute-done((s32[32,8]{0,1:T(8,128)S(1)}, s32[32,8]{0,1:T(8,128)S(1)}, u32[]{:S(2)}, u32[]{:S(2)}) %collective-permute-start.9) | collective-permute-done | bytes 1056 | tf_op jit(solution)/shard_map/ppermute | solution.py:20
  117.5 7.2 %collective-permute-done.10 = s32[32,8]{0,1:T(8,128)S(1)} collective-permute-done((s32[32,8]{0,1:T(8,128)S(1)}, s32[32,8]{0,1:T(8,128)S(1)}, u32[]{:S(2)}, u32[]{:S(2)}) %collective-permute-start.10) | collective-permute-done | bytes 1056 | tf_op jit(solution)/shard_map/ppermute | solution.py:20
  124.7 7.2 %collective-permute-done.11 = s32[32,8]{0,1:T(8,128)S(1)} collective-permute-done((s32[32,8]{0,1:T(8,128)S(1)}, s32[32,8]{0,1:T(8,128)S(1)}, u32[]{:S(2)}, u32[]{:S(2)}) %collective-permute-start.11) | collective-permute-done | bytes 1056 | tf_op jit(solution)/shard_map/ppermute | solution.py:20
  131.9 7.4 %collective-permute-done.12 = s32[32,8]{0,1:T(8,128)S(1)} collective-permute-done((s32[32,8]{0,1:T(8,128)S(1)}, s32[32,8]{0,1:T(8,128)S(1)}, u32[]{:S(2)}, u32[]{:S(2)}) %collective-permute-start.12) | collective-permute-done | bytes 1056 | tf_op jit(solution)/shard_map/ppermute | solution.py:20
  139.4 0.1 reshape.7
  139.5 7.2 %collective-permute-done.13 = s32[32,8]{0,1:T(8,128)S(1)} collective-permute-done((s32[32,8]{0,1:T(8,128)S(1)}, s32[32,8]{0,1:T(8,128)S(1)}, u32[]{:S(2)}, u32[]{:S(2)}) %collective-permute-start.13) | collective-permute-done | bytes 1056 | tf_op jit(solution)/shard_map/ppermute | solution.py:20
  146.8 0.8 dynamic_update_slice.48
  147.6 0.3 dynamic_update_slice.49
  147.8 0.2 dynamic_update_slice.50
  148.1 0.2 dynamic_update_slice.51
  148.3 0.2 dynamic_update_slice.52
  148.5 0.3 dynamic_update_slice.53
  148.8 0.3 dynamic_update_slice.54
  149.1 0.3 dynamic_update_slice.55
  149.4 0.2 dynamic_update_slice.56
  149.6 0.3 dynamic_update_slice.57
  149.9 0.3 dynamic_update_slice.58
  150.2 0.3 dynamic_update_slice.59
  150.5 0.2 dynamic_update_slice.60
  150.8 0.3 dynamic_update_slice.61
  151.1 0.3 dynamic_update_slice.62
  151.4 2.7 collective-permute-done.14
  154.1 0.2 dynamic_update_slice.63
  154.3 9.4 %fusion.25 = bf16[512,1024]{1,0:T(8,128)(2,1)} fusion(bf16[512,3584]{1,0:T(8,128)(2,1)} %all-gather.4.cloned.1.call-done, bf16[1,3584,1024]{2,1,0:T(8,128)(2,1)} %param.12), kind=kOutput, calls=%fused_computation.32 | convolution fusion | flops 3758620672 | bytes 12058624 | tf_op jit(solution)/shard_map/dot_general | solution.py:27
  163.7 7.5 %fusion.22 = bf16[512,1024]{1,0:T(8,128)(2,1)} fusion(bf16[512,3584]{1,0:T(8,128)(2,1)S(1)} %copy-done, bf16[1,3584,1024]{2,1,0:T(8,128)(2,1)} %param.11), kind=kOutput, calls=%fused_computation.31 | convolution fusion | flops 3758620672 | bytes 12058624 | tf_op jit(solution)/shard_map/dot_general | solution.py:26
  171.2 9.1 %multiply_convert_fusion.1 = bf16[512,1024]{1,0:T(8,128)(2,1)} fusion(f32[512]{0:T(512)S(1)} %select_reduce_fusion, bf16[512,3584]{1,0:T(8,128)(2,1)} %all-gather.6.cloned.1.call-done, bf16[1,3584,1024]{2,1,0:T(8,128)(2,1)} %param.13), kind=kOutput, calls=%fused_computation.30 | convolution fusion | flops 3759144960 | bytes 12060672 | tf_op jit(solution)/shard_map/dot_general | solution.py:28
  180.3 0.2 reduce-scatter.3.cloned.1.call-start
  180.5 22.3 %all-reduce.3.cloned.1.call-done = (bf16[512,1024]{1,0:T(8,128)(2,1)}, bf16[512,1024]{1,0:T(8,128)(2,1)}, bf16[512,1024]{1,0:T(8,128)(2,1)}) async-done(((bf16[512,1024]{1,0:T(8,128)(2,1)}, bf16[512,1024]{1,0:T(8,128)(2,1)}, bf16[512,1024]{1,0:T(8,128)(2,1)}), (bf16[512,1024]{1,0:T(8,128)(2,1)}, bf16[512,1024]{1,0:T(8,128)(2,1)}, bf16[512,1024]{1,0:T(8,128)(2,1)})) %all-reduce.3.cloned.1.call-update) | async-done | bytes 3145744 | tf_op jit(solution)/shard_map/psum | solution.py:30
  202.8 9.8 %multiply_convert_fusion = bf16[512,3584]{1,0:T(8,128)(2,1)} fusion(f32[512]{0:T(512)S(1)} %select_reduce_fusion, bf16[1,3584,1024]{2,1,0:T(8,128)(2,1)} %param.13, bf16[512,1024]{1,0:T(8,128)(2,1)} %get-tuple-element.2, bf16[512,1024]{1,0:T(8,128)(2,1)} %get-tuple-element.3), kind=kOutput, calls=%fused_computation.13 | convolution fusion | flops 3765960704 | bytes 13109248 | tf_op jit(solution)/shard_map/dot_general | solution.py:37
  212.7 0.0 reduce-scatter.5.cloned.1.call-start
  212.8 11.6 %fusion.8 = f32[512,3584]{1,0:T(8,128)} fusion(bf16[1,3584,1024]{2,1,0:T(8,128)(2,1)} %param.11, bf16[512,1024]{1,0:T(8,128)(2,1)} %get-tuple-element.2, bf16[512,1024]{1,0:T(8,128)(2,1)} %get-tuple-element.4, bf16[512,1024]{1,0:T(8,128)(2,1)} %get-tuple-element.3), kind=kOutput, calls=%fused_computation.8 | convolution fusion | flops 3764912128 | bytes 17825792 | tf_op jit(solution)/shard_map/dot_general | solution.py:40
  224.4 8.3 %select_convert_fusion = bf16[512,3584]{1,0:T(8,128)(2,1)} fusion(f32[512,3584]{1,0:T(8,128)} %fusion.8, pred[512]{0:T(512)(128)(4,1)S(1)} %get-tuple-element.5, bf16[1,3584,1024]{2,1,0:T(8,128)(2,1)S(1)} %bitcast.33, bf16[512,1024]{1,0:T(8,128)(2,1)S(1)} %copy-done.1, bf16[512,1024]{1,0:T(8,128)(2,1)S(1)} %copy-done.2), kind=kOutput, calls=%fused_computation.12 | convolution fusion | flops 3767795712 | bytes 20447744 | tf_op jit(solution)/shard_map/dot_general | solution.py:42
  232.7 67.0 %reduce-scatter.3.cloned.1.call-done = bf16[32,3584]{1,0:T(8,128)(2,1)} async-done(((bf16[512,3584]{1,0:T(8,128)(2,1)}), bf16[32,3584]{1,0:T(8,128)(2,1)}) %reduce-scatter.3.cloned.1.call-update) | async-done | bytes 229392 | tf_op jit(solution)/shard_map/reduce_scatter | solution.py:44
  299.8 87.3 %reduce-scatter.5.cloned.1.call-done = bf16[32,3584]{1,0:T(8,128)(2,1)} async-done(((bf16[512,3584]{1,0:T(8,128)(2,1)}), bf16[32,3584]{1,0:T(8,128)(2,1)}) %reduce-scatter.5.cloned.1.call-update) | async-done | bytes 229392 | tf_op jit(solution)/shard_map/reduce_scatter | solution.py:45
  (36 shorter events, 0.2 us)
Async XLA Ops:
  7.2 147.2 %all-gather.4.cloned.1.call-start = ((), (), s32[]{:S(2)}) async-start(), calls=%async_computation.2 | async-start | bytes 3899392 | tf_op jit(solution)/shard_map/all_gather | solution.py:13
  7.9 163.3 %all-gather.6.cloned.1.call-start = ((), (), s32[]{:S(2)}) async-start(), calls=%async_computation.4 | async-start | bytes 3899392 | tf_op jit(solution)/shard_map/all_gather | solution.py:14
  8.6 194.2 %all-reduce.3.cloned.1.call-start = ((), (), s32[]{:S(2)}) async-start(), calls=%async_computation.6 | async-start | bytes 6291456 | tf_op jit(solution)/shard_map/psum | solution.py:30
  8.7 43.5 %collective-permute-start = (s32[32,8]{0,1:T(8,128)}, s32[32,8]{0,1:T(8,128)S(1)}, u32[]{:S(2)}, u32[]{:S(2)}) collective-permute-start(s32[32,8]{0,1:T(8,128)} %param.9), channel_id=1, source_target_pairs={{0,2},{2,4},{4,6},{6,8},{8,10},{10,12},{12,14},{14,16},{16,18},{18... | collective-permute-start | bytes 3080 | tf_op jit(solution)/shard_map/ppermute | solution.py:20
  52.2 7.2 %collective-permute-start.1 = (s32[32,8]{0,1:T(8,128)S(1)}, s32[32,8]{0,1:T(8,128)S(1)}, u32[]{:S(2)}, u32[]{:S(2)}) collective-permute-start(s32[32,8]{0,1:T(8,128)S(1)} %collective-permute-done), channel_id=1, source_target_pairs={{0,2},{2,4},{4,6},{6,8},{8,10},{10,12},{12,14},{14,16},{16,18},{18... | collective-permute-start | bytes 3080 | tf_op jit(solution)/shard_map/ppermute | solution.py:20
  59.4 7.3 %collective-permute-start.2 = (s32[32,8]{0,1:T(8,128)S(1)}, s32[32,8]{0,1:T(8,128)S(1)}, u32[]{:S(2)}, u32[]{:S(2)}) collective-permute-start(s32[32,8]{0,1:T(8,128)S(1)} %collective-permute-done.1), channel_id=1, source_target_pairs={{0,2},{2,4},{4,6},{6,8},{8,10},{10,12},{12,14},{14,16},{16,18},{18... | collective-permute-start | bytes 3080 | tf_op jit(solution)/shard_map/ppermute | solution.py:20
  66.7 7.4 %collective-permute-start.3 = (s32[32,8]{0,1:T(8,128)S(1)}, s32[32,8]{0,1:T(8,128)S(1)}, u32[]{:S(2)}, u32[]{:S(2)}) collective-permute-start(s32[32,8]{0,1:T(8,128)S(1)} %collective-permute-done.2), channel_id=1, source_target_pairs={{0,2},{2,4},{4,6},{6,8},{8,10},{10,12},{12,14},{14,16},{16,18},{18... | collective-permute-start | bytes 3080 | tf_op jit(solution)/shard_map/ppermute | solution.py:20
  74.2 7.2 %collective-permute-start.4 = (s32[32,8]{0,1:T(8,128)S(1)}, s32[32,8]{0,1:T(8,128)S(1)}, u32[]{:S(2)}, u32[]{:S(2)}) collective-permute-start(s32[32,8]{0,1:T(8,128)S(1)} %collective-permute-done.3), channel_id=1, source_target_pairs={{0,2},{2,4},{4,6},{6,8},{8,10},{10,12},{12,14},{14,16},{16,18},{18... | collective-permute-start | bytes 3080 | tf_op jit(solution)/shard_map/ppermute | solution.py:20
  81.4 7.2 %collective-permute-start.5 = (s32[32,8]{0,1:T(8,128)S(1)}, s32[32,8]{0,1:T(8,128)S(1)}, u32[]{:S(2)}, u32[]{:S(2)}) collective-permute-start(s32[32,8]{0,1:T(8,128)S(1)} %collective-permute-done.4), channel_id=1, source_target_pairs={{0,2},{2,4},{4,6},{6,8},{8,10},{10,12},{12,14},{14,16},{16,18},{18... | collective-permute-start | bytes 3080 | tf_op jit(solution)/shard_map/ppermute | solution.py:20
  88.6 7.2 %collective-permute-start.6 = (s32[32,8]{0,1:T(8,128)S(1)}, s32[32,8]{0,1:T(8,128)S(1)}, u32[]{:S(2)}, u32[]{:S(2)}) collective-permute-start(s32[32,8]{0,1:T(8,128)S(1)} %collective-permute-done.5), channel_id=1, source_target_pairs={{0,2},{2,4},{4,6},{6,8},{8,10},{10,12},{12,14},{14,16},{16,18},{18... | collective-permute-start | bytes 3080 | tf_op jit(solution)/shard_map/ppermute | solution.py:20
  95.8 7.2 %collective-permute-start.7 = (s32[32,8]{0,1:T(8,128)S(1)}, s32[32,8]{0,1:T(8,128)S(1)}, u32[]{:S(2)}, u32[]{:S(2)}) collective-permute-start(s32[32,8]{0,1:T(8,128)S(1)} %collective-permute-done.6), channel_id=1, source_target_pairs={{0,2},{2,4},{4,6},{6,8},{8,10},{10,12},{12,14},{14,16},{16,18},{18... | collective-permute-start | bytes 3080 | tf_op jit(solution)/shard_map/ppermute | solution.py:20
  103.0 7.2 %collective-permute-start.8 = (s32[32,8]{0,1:T(8,128)S(1)}, s32[32,8]{0,1:T(8,128)S(1)}, u32[]{:S(2)}, u32[]{:S(2)}) collective-permute-start(s32[32,8]{0,1:T(8,128)S(1)} %collective-permute-done.7), channel_id=1, source_target_pairs={{0,2},{2,4},{4,6},{6,8},{8,10},{10,12},{12,14},{14,16},{16,18},{18... | collective-permute-start | bytes 3080 | tf_op jit(solution)/shard_map/ppermute | solution.py:20
  110.2 7.3 %collective-permute-start.9 = (s32[32,8]{0,1:T(8,128)S(1)}, s32[32,8]{0,1:T(8,128)S(1)}, u32[]{:S(2)}, u32[]{:S(2)}) collective-permute-start(s32[32,8]{0,1:T(8,128)S(1)} %collective-permute-done.8), channel_id=1, source_target_pairs={{0,2},{2,4},{4,6},{6,8},{8,10},{10,12},{12,14},{14,16},{16,18},{18... | collective-permute-start | bytes 3080 | tf_op jit(solution)/shard_map/ppermute | solution.py:20
  117.5 7.2 %collective-permute-start.10 = (s32[32,8]{0,1:T(8,128)S(1)}, s32[32,8]{0,1:T(8,128)S(1)}, u32[]{:S(2)}, u32[]{:S(2)}) collective-permute-start(s32[32,8]{0,1:T(8,128)S(1)} %collective-permute-done.9), channel_id=1, source_target_pairs={{0,2},{2,4},{4,6},{6,8},{8,10},{10,12},{12,14},{14,16},{16,18},{18... | collective-permute-start | bytes 3080 | tf_op jit(solution)/shard_map/ppermute | solution.py:20
  124.7 7.2 %collective-permute-start.11 = (s32[32,8]{0,1:T(8,128)S(1)}, s32[32,8]{0,1:T(8,128)S(1)}, u32[]{:S(2)}, u32[]{:S(2)}) collective-permute-start(s32[32,8]{0,1:T(8,128)S(1)} %collective-permute-done.10), channel_id=1, source_target_pairs={{0,2},{2,4},{4,6},{6,8},{8,10},{10,12},{12,14},{14,16},{16,18},{18... | collective-permute-start | bytes 3080 | tf_op jit(solution)/shard_map/ppermute | solution.py:20
  131.9 7.4 %collective-permute-start.12 = (s32[32,8]{0,1:T(8,128)S(1)}, s32[32,8]{0,1:T(8,128)S(1)}, u32[]{:S(2)}, u32[]{:S(2)}) collective-permute-start(s32[32,8]{0,1:T(8,128)S(1)} %collective-permute-done.11), channel_id=1, source_target_pairs={{0,2},{2,4},{4,6},{6,8},{8,10},{10,12},{12,14},{14,16},{16,18},{18... | collective-permute-start | bytes 3080 | tf_op jit(solution)/shard_map/ppermute | solution.py:20
  139.3 7.4 %collective-permute-start.13 = (s32[32,8]{0,1:T(8,128)S(1)}, s32[32,8]{0,1:T(8,128)S(1)}, u32[]{:S(2)}, u32[]{:S(2)}) collective-permute-start(s32[32,8]{0,1:T(8,128)S(1)} %collective-permute-done.12), channel_id=1, source_target_pairs={{0,2},{2,4},{4,6},{6,8},{8,10},{10,12},{12,14},{14,16},{16,18},{18... | collective-permute-start | bytes 3080 | tf_op jit(solution)/shard_map/ppermute | solution.py:20
  146.8 7.3 %collective-permute-start.14 = (s32[32,8]{0,1:T(8,128)S(1)}, s32[32,8]{0,1:T(8,128)S(1)}, u32[]{:S(2)}, u32[]{:S(2)}) collective-permute-start(s32[32,8]{0,1:T(8,128)S(1)} %collective-permute-done.13), channel_id=1, source_target_pairs={{0,2},{2,4},{4,6},{6,8},{8,10},{10,12},{12,14},{14,16},{16,18},{18... | collective-permute-start | bytes 3080 | tf_op jit(solution)/shard_map/ppermute | solution.py:20
  154.3 9.4 %copy-start = (bf16[512,3584]{1,0:T(8,128)(2,1)S(1)}, bf16[512,3584]{1,0:T(8,128)(2,1)}, u32[]{:S(2)}) copy-start(bf16[512,3584]{1,0:T(8,128)(2,1)} %all-gather.4.cloned.1.call-done) | copy-start | bytes 11010052
  180.3 119.4 %reduce-scatter.3.cloned.1.call-start = ((), (), s32[]{:S(2)}) async-start(), calls=%async_computation.3 | async-start | bytes 3899392 | tf_op jit(solution)/shard_map/reduce_scatter | solution.py:44
  212.7 11.7 %slice-start = ((s8[7340032]{0:T(1024)(128)(4,1)}), s8[3145728]{0:T(1024)(128)(4,1)S(1)}, s32[]{:S(2)}) async-start(s8[7340032]{0:T(1024)(128)(4,1)} %bitcast.32), calls=%async_computation.7 | async-start | bytes 6291456
  212.7 174.3 %reduce-scatter.5.cloned.1.call-start = ((), (), s32[]{:S(2)}) async-start(), calls=%async_computation.5 | async-start | bytes 3899392 | tf_op jit(solution)/shard_map/reduce_scatter | solution.py:45
  212.8 11.6 %slice-start.1 = ((s8[7340032]{0:T(1024)(128)(4,1)}), s8[4194304]{0:T(1024)(128)(4,1)S(1)}, s32[]{:S(2)}) async-start(s8[7340032]{0:T(1024)(128)(4,1)} %bitcast.32), calls=%async_computation.8 | async-start | bytes 8388608
  212.8 11.6 %copy-start.1 = (bf16[512,1024]{1,0:T(8,128)(2,1)S(1)}, bf16[512,1024]{1,0:T(8,128)(2,1)}, u32[]{:S(2)}) copy-start(bf16[512,1024]{1,0:T(8,128)(2,1)} %get-tuple-element.3) | copy-start | bytes 3145732
  212.8 11.6 %copy-start.2 = (bf16[512,1024]{1,0:T(8,128)(2,1)S(1)}, bf16[512,1024]{1,0:T(8,128)(2,1)}, u32[]{:S(2)}) copy-start(bf16[512,1024]{1,0:T(8,128)(2,1)} %get-tuple-element.4) | copy-start | bytes 3145732
Sparse Core Ops, SparseCore 0:
  10.7 74.8 all-gather.3
  88.4 70.3 all-gather.5
  180.4 22.3 all-reduce.2
  212.8 86.8 reduce-scatter.2
  302.5 84.5 reduce-scatter.4
